TPU v7x, 512 devices: a whole 4x4x16 slice. The times are simulated.
512 devices in a mesh: gx: 16 (over y_lo, x, core), gy: 32 (over y_hi, z).
Axes of the slice: x: 4, y: 4 (y_hi: 2, y_lo: 2; y = y_hi * 2 + y_lo), z: 16, core: 2. Of those that a mesh axis runs over, the one named last changes fastest.
Arguments:
- phase_field: float32 [16, 2048, 2048], P(None, 'gy', 'gx'), may hold values from -1 to 1
- mobility: float32 [16, 2048, 2048], P(None, 'gy', 'gx'), may hold values from 0.25 to 2.5
- x_inverse: bfloat16 [2048, 2048], P('gx'), may hold values from -2 to 2
- y_inverse: bfloat16 [2048, 2048], P('gy'), may hold values from -2 to 2
Outputs:
- new_phase: float32 [16, 2048, 2048], P(None, 'gy', 'gx')
All inputs are finite; a program needn't handle non-finite values.
Results may differ from a plain program's by a relative error of at most 0.0041.
Values may be sent and summed in bfloat16 or wider, within the bound.
No kernel may reach another device: no remote copies, remote signals or barrier semaphores. Data moves between devices by JAX's collectives and lax.ppermute only.
A program may use at most 64 MiB of HBM per device.

v0:
```python
import jax
import jax.numpy as jnp
from jax import lax
from jax.experimental import pallas as pl
from jax.experimental.pallas import tpu as pltpu
from jax.sharding import Mesh
from jax.sharding import PartitionSpec as P

GX = ("yl", "x", "c")
GY = ("yh", "z")

step_size = 0.15
F32 = jnp.float32
BF16 = jnp.bfloat16
NT = (((1,), (1,)), ((), ()))
VMEM = pl.BlockSpec(memory_space=pltpu.VMEM)
OFF = 8


def near(v):
    return pltpu.with_memory_space_constraint(v, pltpu.VMEM)


def away(v):
    return pltpu.with_memory_space_constraint(v, pltpu.HBM)


def kept(shape, dtype):
    return pltpu.VMEM(shape, dtype)


FAR = pl.BlockSpec(memory_space=pltpu.HBM)


def away_kept(shape, dtype):
    return pltpu.HBM(shape, dtype)


def call(kernel, out_shape, args, scalar=None, scratch=(), far=(), far_out=(), aliases=None):
    scalars = [] if scalar is None else [scalar]
    many = isinstance(out_shape, tuple)
    return pl.pallas_call(
        kernel,
        out_shape=out_shape,
        in_specs=[pl.BlockSpec(memory_space=pltpu.SMEM)] * len(scalars) + [FAR if i in far else VMEM for i in range(len(args))],
        out_specs=tuple(FAR if i in far_out else VMEM for i in range(len(out_shape))) if many else VMEM,
        scratch_shapes=list(scratch),
        input_output_aliases=aliases or {},
        compiler_params=pltpu.CompilerParams(vmem_limit_bytes=16 << 20),
    )(*scalars, *[away(v) if i in far else near(v) for i, v in enumerate(args)])


def face_mob(p, q):
    return 2.0 * p * q / jnp.maximum(p + q, 0.25)


def turn(x, shift, axis):
    return pltpu.roll(x, shift % x.shape[axis], axis)


def places(shape, axis):
    return lax.broadcasted_iota(jnp.int32, shape, axis)


def pack_x_kernel(core_ref, p_hbm, m_hbm, x_hbm, y_hbm, left_ref, right_ref, p_ref, m_ref, rows_hbm, part_hbm, x_ref, part_ref, sems):
    planes, _, cx = p_ref.shape
    pairs = planes // 2
    rows = part_hbm.shape[0]
    copies = (
        (y_hbm.at[pl.ds(pl.multiple_of(core_ref[0] * rows, rows), rows)], part_ref),
        (p_hbm, p_ref),
        (m_hbm, m_ref),
        (x_hbm, x_ref),
    )
    copies = [pltpu.make_async_copy(src, dst, sems.at[i]) for i, (src, dst) in enumerate(copies)]
    for copy in copies:
        copy.start()
    copies[0].wait()
    out = pltpu.make_async_copy(part_ref, part_hbm, sems.at[0])
    out.start()
    copies[3].wait()
    own = pltpu.make_async_copy(x_ref, rows_hbm.at[pl.ds(0, cx)], sems.at[3])
    own.start()
    for a, ref in enumerate((p_ref, m_ref)):
        copies[1 + a].wait()
        for i in range(pairs):
            t = jnp.concatenate([ref[i], ref[i + pairs]], axis=0).T
            for j in range(2):
                k = (2 * a + j) * pairs + i
                left_ref[k : k + 1, :] = t[j : j + 1]
                right_ref[k : k + 1, :] = t[cx - 2 + j : cx - 1 + j]
    base = 4 * pairs
    first = x_ref[0:16, :][0:1].astype(F32)
    last = x_ref[cx - 16 : cx, :][15:16].astype(F32)
    for s in range(16):
        left_ref[base + s : base + s + 1, :] = first[:, s * cx : (s + 1) * cx]
        right_ref[base + s : base + s + 1, :] = last[:, s * cx : (s + 1) * cx]
    out.wait()
    own.wait()


def strip(x, cy):
    both = jnp.concatenate([turn(x, OFF, 1), turn(x, OFF - cy, 1)], axis=0)
    lane = places(both.shape, 1)
    return jnp.where((lane >= OFF) & (lane < OFF + cy), both, 0.0)


def received(left_ref, right_ref, a, pairs, cy):
    refs = ((left_ref, 2 * a), (left_ref, 2 * a + 1), (right_ref, 2 * a), (right_ref, 2 * a + 1))
    return [strip(ref[k * pairs : (k + 1) * pairs, :], cy) for ref, k in refs]


def pack_y_kernel(
    p_ref, m_ref, own_l_ref, own_r_ref, left_ref, right_ref, _, up_ref, down_ref, rows_hbm, row_ref, cast_ref, sem
):
    planes, cy, cx = p_ref.shape
    base = left_ref.shape[0] - 16
    row_ref[...] = jnp.zeros(row_ref.shape, F32)
    for j, ref in enumerate((left_ref, own_l_ref, own_r_ref, right_ref)):
        for s in range(16):
            row_ref[j : j + 1, s * cx : (s + 1) * cx] = ref[base + s : base + s + 1, :]
    cast_ref[...] = row_ref[...].astype(BF16)
    copy = pltpu.make_async_copy(cast_ref, rows_hbm.at[pl.ds(cx, 16)], sem)
    copy.start()
    for a, ref in enumerate((p_ref, m_ref)):
        for r in range(3):
            up_ref[3 * a + r] = ref[:, cy - 3 + r, :]
            down_ref[3 * a + r] = ref[:, r, :]
    lane = places((planes, cx), 1)
    up = jnp.zeros((planes, cx), F32)
    down = up
    for a in range(2):
        for j, s in enumerate(received(left_ref, right_ref, a, planes // 2, cy)):
            at = 3 * (4 * a + j)
            here = (lane >= at) & (lane < at + 3)
            up = jnp.where(here, turn(s, at - (OFF + cy - 3), 1), up)
            down = jnp.where(here, turn(s, at - OFF, 1), down)
    up_ref[6] = up
    down_ref[6] = down
    copy.wait()


def explicit_kernel(
    p_ref, m_ref, own_l_ref, own_r_ref, left_ref, right_ref, up_ref, down_ref,
    send_hbm, fz_ref, fy_ref, fx_ref, edge_ref,
    v_ref, c_ref, f_ref, side_ref, rim_ref, turned_ref, quarter_ref, sems,
):
    planes, cy, cx = p_ref.shape
    pairs = planes // 2
    tall = cy + 2 * OFF
    lane = places((planes, cx), 1)
    plane = places((planes, cx), 0)

    def strips(a):
        out = []
        for j, s in enumerate(received(left_ref, right_ref, a, pairs, cy)):
            at = 3 * (4 * a + j)
            s = jnp.where((lane >= OFF - 3) & (lane < OFF), turn(up_ref[6], OFF - 3 - at, 1), s)
            s = jnp.where((lane >= OFF + cy) & (lane < OFF + cy + 3), turn(down_ref[6], OFF + cy - at, 1), s)
            out.append(s)
        own = []
        for ref, j, at in ((own_l_ref, 0, 0), (own_l_ref, 1, 1), (own_r_ref, 0, cx - 2), (own_r_ref, 1, cx - 1)):
            k = 2 * a + j
            s = strip(ref[k * pairs : (k + 1) * pairs, :], cy)
            for r in (1, 2):
                s = jnp.where(lane == OFF - 3 + r, turn(up_ref[3 * a + r], OFF - 3 + r - at, 1), s)
            for r in (0, 1):
                s = jnp.where(lane == OFF + cy + r, turn(down_ref[3 * a + r], OFF + cy + r - at, 1), s)
            own.append(s)
        return out[:2] + own[:2], own[2:] + out[2:]

    def strip_first(v, m, vl, ml, vr, mr):
        above = jnp.where(plane == planes - 1, 0.0, turn(m, -1, 0))
        fz = face_mob(m, above)
        gz = fz * (turn(v, -1, 0) - v)
        fy = face_mob(m, turn(m, -1, 1))
        gy = fy * (turn(v, -1, 1) - v)
        lap = gz - jnp.where(plane == 0, 0.0, turn(gz, 1, 0)) + gy - turn(gy, 1, 1)
        lap = lap + face_mob(m, mr) * (vr - v) + face_mob(m, ml) * (vl - v)
        return v + step_size * lap

    turned_ref[...] = jnp.zeros(turned_ref.shape, F32)
    for side, (v, m) in enumerate(zip(strips(0), strips(1), strict=True)):
        f = face_mob(m[1], m[2])
        a = strip_first(v[1], m[1], v[0], m[0], v[2], m[2])
        b = strip_first(v[2], m[2], v[1], m[1], v[3], m[3])
        turned_ref[pl.ds(2 - side, planes, stride=2), :] = f * (v[2] - v[1])
        turned_ref[pl.ds(66 - side, planes, stride=2), :] = f * (b - a)
        side_ref[...] = f
        even = turn(side_ref[pl.ds(0, pairs, stride=2), :], -OFF, 1)
        odd = turn(side_ref[pl.ds(1, pairs, stride=2), :], cy - OFF, 1)
        edge_ref[side * pairs : (side + 1) * pairs, :] = jnp.where(lane[:pairs] < cy, even, odd)
    across = turned_ref[...].T

    def ends(k, z):
        return turn(across[:tall], -(64 * k + 2 * z + 2), 1)

    blank = jnp.zeros((OFF, cx), F32)
    for ref in (v_ref, c_ref, f_ref):
        for z in (0, planes + 1):
            ref[z * tall : (z + 1) * tall, :] = jnp.zeros((tall, cx), F32)
    for ref, a, field in ((v_ref, 0, p_ref), (c_ref, 1, m_ref)):
        for z in range(planes):
            base = (z + 1) * tall
            ref[base : base + OFF, :] = blank
            ref[base + OFF : base + OFF + cy, :] = field[z]
            ref[base + OFF + cy : base + tall, :] = blank
        for r in range(3):
            ref[pl.ds(tall + OFF - 3 + r, planes, stride=tall), :] = up_ref[3 * a + r]
            ref[pl.ds(tall + OFF + cy + r, planes, stride=tall), :] = down_ref[3 * a + r]

    wide = places((tall, cx), 1)

    def step(v, above, fz, fy, fx, gz_before, end):
        gz = fz * (above - v)
        gy = fy * (turn(v, -1, 0) - v)
        gx = jnp.where(wide == 0, end, fx * (v - turn(v, 1, 1)))
        lap = gz - gz_before + gy - turn(gy, 1, 0)
        lap = lap + jnp.where(wide == cx - 1, end, turn(gx, -1, 1)) - gx
        return v + step_size * lap, gz

    fz_ref[:tall, :] = jnp.zeros((tall, cx), F32)
    fy_ref[:OFF, :] = jnp.zeros((OFF, cx), F32)
    before = jnp.zeros((tall, cx), F32)
    for z in range(planes):
        here, above = pl.ds((z + 1) * tall, tall), pl.ds((z + 2) * tall, tall)
        m = c_ref[here, :]
        fz = face_mob(m, c_ref[above, :])
        fy = face_mob(m, turn(m, -1, 0))
        fx = face_mob(m, turn(m, 1, 1))
        fz_ref[here, :] = fz
        fy_ref[pl.ds(OFF + z * tall, tall), :] = fy
        fx_ref[pl.ds(z * tall, tall), :] = fx
        out, before = step(v_ref[here, :], v_ref[above, :], fz, fy, fx, before, ends(0, z))
        f_ref[here, :] = out

    rim_ref[...] = jnp.zeros(rim_ref.shape, F32)
    quarter = planes // 4
    before = jnp.zeros((tall, cx), F32)
    copies = []
    for z in range(planes):
        here, above = pl.ds((z + 1) * tall, tall), pl.ds((z + 2) * tall, tall)
        fy, fx = fy_ref[pl.ds(OFF + z * tall, tall), :], fx_ref[pl.ds(z * tall, tall), :]
        out, before = step(f_ref[here, :], f_ref[above, :], fz_ref[here, :], fy, fx, before, ends(1, z))
        q, row = z // quarter, z % quarter
        quarter_ref[q, row * cy : (row + 1) * cy, :] = out[OFF : OFF + cy].astype(BF16)
        rim_ref[q, 2 * row : 2 * row + 1, :] = out[OFF - 1 : OFF]
        rim_ref[q, 2 * row + 1 : 2 * row + 2, :] = out[OFF + cy : OFF + cy + 1]
        if row == quarter - 1:
            quarter_ref[q, quarter * cy :, :] = rim_ref[q].astype(BF16)
            for x in range(4):
                to = send_hbm.at[(q // 2) * 8 + x * 2 + q % 2]
                copies.append(pltpu.make_async_copy(quarter_ref.at[q], to, sems.at[q, x]))
                copies[-1].start()
    for copy in copies:
        copy.wait()


def solve_x_kernel(block_ref, got_ref, x0_hbm, x1_hbm, x2_hbm, x3_hbm, out_ref, x0_ref, x1_ref, x2_ref, x3_ref, sems):
    own = block_ref[0]
    parts, lines, cx = got_ref.shape
    main = lines - 16
    moves = ((x0_hbm, x0_ref), (x1_hbm, x1_ref), (x2_hbm, x2_ref), (x3_hbm, x3_ref))
    copies = [pltpu.make_async_copy(src, dst, sems.at[i]) for i, (src, dst) in enumerate(moves)]
    for copy in copies:
        copy.start()
    a = jnp.concatenate([got_ref[s] for s in range(parts)], axis=1)
    for copy in copies:
        copy.wait()
    for other, x_ref in enumerate((x0_ref, x1_ref, x2_ref, x3_ref)):
        block = own ^ other
        m = lax.dot_general(a, x_ref[:cx], NT, preferred_element_type=F32)
        out_ref[block, : main + 8] = m[: main + 8]
        e = lax.dot_general(x_ref[cx:], a[:main], NT, preferred_element_type=F32)
        out_ref[block, main + 8 : main + 12] = e[:4, :cx]
        out_ref[block, main + 12 :] = e[:4, cx:]


def implicit_kernel(back_ref, fz_ref, fy_ref, fx_ref, edge_ref, out_ref, c_ref, e_ref):
    planes, cy, cx = out_ref.shape
    tall = cy + 2 * OFF
    quarter, pairs = planes // 4, planes // 2
    main = quarter * cy

    def chemical(s):
        return s * s * s - s

    for z in (0, planes + 1):
        c_ref[z * tall : (z + 1) * tall, :] = jnp.zeros((tall, cx), F32)
    for q in range(4):
        e_ref[q * 8 : (q + 1) * 8, :] = chemical(back_ref[q, main + 8 : main + 16])
        rims = chemical(back_ref[q, main : main + 8])
        for at in range(quarter):
            base = (q * quarter + at + 1) * tall
            c_ref[base + OFF : base + OFF + cy, :] = chemical(back_ref[q, at * cy : (at + 1) * cy])
            c_ref[base + OFF - 1 : base + OFF, :] = rims[2 * at : 2 * at + 1]
            c_ref[base + OFF + cy : base + OFF + cy + 1, :] = rims[2 * at + 1 : 2 * at + 2]
    ends = [e_ref[pl.ds(j, pairs, stride=4), :] for j in range(4)]
    left = edge_ref[:pairs, :] * (ends[1] - ends[0])
    right = edge_ref[pairs:, :] * (ends[3] - ends[2])
    across = jnp.concatenate([left, right, jnp.zeros((cx - planes, cx), F32)], axis=0).T
    lane = places((cy, cx), 1)
    before = jnp.zeros((cy, cx), F32)
    for z in range(planes):
        base = (z + 1) * tall + OFF
        flat = z * tall + OFF
        c = c_ref[base : base + cy, :]
        gz = fz_ref[base : base + cy, :] * (c_ref[base + tall : base + tall + cy, :] - c)
        gy = fy_ref[flat + OFF : flat + OFF + cy, :] * (c_ref[base + 1 : base + 1 + cy, :] - c)
        gu = fy_ref[flat + OFF - 1 : flat + OFF - 1 + cy, :] * (c - c_ref[base - 1 : base - 1 + cy, :])
        rows = slice((z % 2) * cy, (z % 2 + 1) * cy)
        gl = jnp.broadcast_to(across[rows, z // 2 : z // 2 + 1], (cy, cx))
        gr = jnp.broadcast_to(across[rows, pairs + z // 2 : pairs + z // 2 + 1], (cy, cx))
        gx = jnp.where(lane == 0, gl, fx_ref[flat : flat + cy, :] * (c - turn(c, 1, 1)))
        lap = gz - before + gy - gu + jnp.where(lane == cx - 1, gr, turn(gx, -1, 1)) - gx
        s = back_ref[z // quarter, (z % quarter) * cy : (z % quarter + 1) * cy]
        out_ref[z] = (s + step_size * lap).astype(BF16)
        before = gz


def solve_y_near_kernel(side_ref, y_hbm, u_ref, sum_ref, y_ref, near_ref, sems):
    high = side_ref[0]
    half, _ = u_ref.shape
    halves = (high, 1 - high)
    columns = [y_hbm.at[:, pl.ds(pl.multiple_of(h * half, half), half)] for h in halves]
    copies = [pltpu.make_async_copy(c, ref, sems.at[i]) for i, (c, ref) in enumerate(zip(columns, (near_ref, y_ref), strict=True))]
    for copy in copies:
        copy.start()
    copies[0].wait()
    sum_ref[...] = jnp.dot(near_ref[...], u_ref[...], preferred_element_type=F32)
    copies[1].wait()


def solve_y_far_kernel(sum_ref, y_ref, u_ref, out_ref):
    total = sum_ref[...] + jnp.dot(y_ref[...], u_ref[...], preferred_element_type=F32)
    out_ref[...] = total.astype(BF16)


def pack_x(core, p, m, x_inverse, y_inverse):
    cx = p.shape[2]
    shape = (2 * p.shape[0] + 16, cx)
    cy, order = y_inverse.shape
    out = (kept(shape, F32),) * 2 + (kept(p.shape, F32),) * 2 + (away_kept((cx + 16, order), BF16),)
    out += (away_kept((cy // 2, order), BF16),)
    scratch = (pltpu.VMEM((cx, order), BF16), pltpu.VMEM((cy // 2, order), BF16), pltpu.SemaphoreType.DMA((4,)))
    return call(pack_x_kernel, out, (p, m, x_inverse, y_inverse), core, scratch, range(4), (4, 5))


def pack_y(p, m, own_l, own_r, left, right, rows):
    order = rows.shape[1]
    out = (kept((7, p.shape[0], p.shape[2]), F32),) * 2 + (away_kept(rows.shape, BF16),)
    scratch = (pltpu.VMEM((16, order), F32), pltpu.VMEM((16, order), BF16), pltpu.SemaphoreType.DMA(()))
    args = (p, m, own_l, own_r, left, right, rows)
    return call(pack_y_kernel, out, args, scratch=scratch, far=(6,), far_out=(2,), aliases={6: 2})


def explicit(*args):
    planes, cy, cx = args[0].shape
    tall = cy + 2 * OFF
    lines = planes // 4 * cy + 16
    field = pltpu.VMEM(((planes + 2) * tall, cx), F32)
    out = (
        away_kept((16, lines, cx), BF16),
        kept(((planes + 1) * tall, cx), F32),
        kept((planes * tall + OFF, cx), F32),
        kept((planes * tall, cx), F32),
        kept((planes, cx), F32),
    )
    scratch = (field, field, field, pltpu.VMEM((planes, cx), F32))
    scratch += (pltpu.VMEM((4, 16, cx), F32), pltpu.VMEM((cx, cx), F32))
    scratch += (pltpu.VMEM((4, lines, cx), BF16), pltpu.SemaphoreType.DMA((4, 4)))
    return call(explicit_kernel, out, args, scratch=scratch, far_out=(0,))


def solve_x(block, got, x_blocks):
    _, lines, cx = got.shape
    blocks = pltpu.VMEM(x_blocks[0].shape, BF16)
    scratch = (blocks,) * 4 + (pltpu.SemaphoreType.DMA((4,)),)
    return call(solve_x_kernel, kept((4, lines, cx), F32), (got, *x_blocks), block, scratch, (1, 2, 3, 4))


def implicit(back, faces, planes, cy):
    cx = back.shape[2]
    tall = cy + 2 * OFF
    scratch = (pltpu.VMEM(((planes + 2) * tall, cx), F32), pltpu.VMEM((32, cx), F32))
    return call(implicit_kernel, kept((planes, cy, cx), BF16), (back, *faces), scratch=scratch)


def solve_y_near(side, y, u):
    half, cx = u.shape
    out = (kept((half, cx), F32), kept((half, half), BF16))
    scratch = (pltpu.VMEM((half, half), BF16), pltpu.SemaphoreType.DMA((2,)))
    return call(solve_y_near_kernel, out, (y, u), side, scratch, (0,))


def solve_y_far(*parts):
    return call(solve_y_far_kernel, kept(parts[-1].shape, BF16), parts)


def both_ways(to_before, to_after, axis):
    size = lax.axis_size(axis)
    up = [(i, i + 1) for i in range(size - 1)]
    return lax.ppermute(to_after, axis, up), lax.ppermute(to_before, axis, [(j, i) for i, j in up])


def local(phase_field, mobility, x_inverse, y_inverse):
    planes, cy, cx = phase_field.shape
    order = y_inverse.shape[1]
    half = order // 2
    core, low, high = lax.axis_index("c"), lax.axis_index("yl"), lax.axis_index("yh")
    swap = [(0, 1), (1, 0)]

    one = lambda v: v.reshape(1).astype(jnp.int32)

    own_l, own_r, phase_field, mobility, rows, y_part = pack_x(one(core), phase_field, mobility, x_inverse, y_inverse)
    y_rows = lax.all_gather(y_part, ("z", "c"), axis=0, tiled=True)
    left, right = both_ways(own_l, own_r, GX)
    to_up, to_down, rows = pack_y(phase_field, mobility, own_l, own_r, left, right, rows)
    up, down = both_ways(to_down, to_up, GY)
    rows_yl = lax.ppermute(rows, "yl", swap)
    x_blocks = (rows, lax.ppermute(rows, "c", swap), rows_yl, lax.ppermute(rows_yl, "c", swap))

    send, *faces = explicit(phase_field, mobility, own_l, own_r, left, right, up, down)
    got = lax.all_to_all(send, GX, 0, 0, tiled=True)
    back = solve_x(one(low * 2 + core), got, x_blocks)
    back = lax.all_to_all(back, ("yl", "c"), 0, 0, tiled=True)
    updated = implicit(back, faces, planes, cy)

    mine = lax.all_to_all(updated, "z", 0, 0, tiled=True).reshape(half, cx)
    y_rows, mine = lax.optimization_barrier((y_rows, mine))
    theirs = lax.ppermute(mine, "yh", swap)
    part, y_far = solve_y_near(one(high), y_rows, mine)
    out = solve_y_far(part, y_far, theirs).reshape(16, cy, cx)
    out = lax.all_to_all(out, "z", 0, 0, tiled=True)
    return out.astype(F32)


def solution(mesh):
    shape = (2, mesh.shape["gx"] // 4, 2, 2, mesh.shape["gy"] // 2)
    torus = Mesh(mesh.devices.reshape(shape), ("yl", "x", "c", "yh", "z"))
    in_specs = (P(None, GY, GX), P(None, GY, GX), P(GX, None), P(GY, None))
    return jax.shard_map(local, mesh=torus, in_specs=in_specs, out_specs=P(None, GY, GX), check_vma=False)
```

profile of v0, /device:TPU:16, one launch (start us, length us, event | category | flops | bytes accessed | tf_op | source)
XLA Modules:
  0.0 151.8 jit_solution(4890515358463316344)
XLA Ops:
  6.5 0.0 all-gather.2.cloned.1.call-start
  6.5 2.2 %shard_map.46 = (f32[48,128]{1,0:T(8,128)S(1)}, f32[48,128]{1,0:T(8,128)S(1)}, f32[16,64,128]{2,1,0:T(8,128)S(1)}, f32[16,64,128]{2,1,0:T(8,128)S(1)}, bf16[144,...) custom-call(s32[1]{0:T(128)} %bitcast.1.core_ref, f32[16,64,128]{2,1,0:T(8,128)} %p_hbm.1, f32[16,64,128]{2,1,0:T(8,128)} %m_hbm.1, ...), custom_call_target="tpu_custom_call" | custom-call | tf_op jit(solution)/shard_map/pallas_call | solution.py:42
  8.8 0.0 all-gather.2.cloned.1.call-update
  8.8 1.7 %collective-permute-start = (f32[48,128]{1,0:T(8,128)S(1)}, f32[48,128]{1,0:T(8,128)S(1)}, u32[]{:S(2)}, u32[]{:S(2)}) collective-permute-start(f32[48,128]{1,0:T(8,128)S(1)} %get-tuple-element.27.own_r_ref), channel_id=1, source_target_pairs={{0,32},{32,64},{64,96},{96,128},{128,160},{160,192},{192,224},{224... | collective-permute-start | bytes 73736 | tf_op jit(solution)/shard_map/ppermute | solution.py:403
  10.6 1.3 collective-permute-start.1
  11.9 0.0 collective-permute-done.left_ref
  11.9 3.1 %collective-permute-done.1.right_ref = f32[48,128]{1,0:T(8,128)S(1)} collective-permute-done((f32[48,128]{1,0:T(8,128)S(1)}, f32[48,128]{1,0:T(8,128)S(1)}, u32[]{:S(2)}, u32[]{:S(2)}) %collective-permute-start.1) | collective-permute-done | bytes 24608 | tf_op jit(solution)/shard_map/ppermute | solution.py:403
  14.9 0.8 shard_map.47
  15.7 6.3 %collective-permute-start.5 = (bf16[144,2048]{1,0:T(8,128)(2,1)}, bf16[144,2048]{1,0:T(8,128)(2,1)}, u32[]{:S(2)}, u32[]{:S(2)}) collective-permute-start(bf16[144,2048]{1,0:T(8,128)(2,1)} %get-tuple-element.32.x0_hbm), channel_id=1, source_target_pairs={{0,256},{256,0},{1,257},{257,1},{2,258},{258,2},{3,259},{259,3},{4... | collective-permute-start | bytes 1769480 | tf_op jit(solution)/shard_map/ppermute | solution.py:420
  22.0 3.8 %collective-permute-start.2 = (f32[7,16,128]{2,1,0:T(8,128)S(1)}, f32[7,16,128]{2,1,0:T(8,128)S(1)}, u32[]{:S(2)}, u32[]{:S(2)}) collective-permute-start(f32[7,16,128]{2,1,0:T(8,128)S(1)} %get-tuple-element.29), channel_id=1, source_target_pairs={{0,1},{1,2},{2,3},{3,4},{4,5},{5,6},{6,7},{7,8},{8,9},{9,10},{10,1... | collective-permute-start | bytes 172040 | tf_op jit(solution)/shard_map/ppermute | solution.py:403
  25.8 9.6 %collective-permute-start.3 = (f32[7,16,128]{2,1,0:T(8,128)S(1)}, f32[7,16,128]{2,1,0:T(8,128)S(1)}, u32[]{:S(2)}, u32[]{:S(2)}) collective-permute-start(f32[7,16,128]{2,1,0:T(8,128)S(1)} %get-tuple-element.30), channel_id=1, source_target_pairs={{1,0},{2,1},{3,2},{4,3},{5,4},{6,5},{7,6},{8,7},{9,8},{10,9},{11,1... | collective-permute-start | bytes 172040 | tf_op jit(solution)/shard_map/ppermute | solution.py:403
  35.4 0.9 collective-permute-done.2.up_ref
  36.4 1.4 collective-permute-done.3.down_ref
  37.8 4.3 %shard_map.48 = (bf16[16,272,128]{2,1,0:T(8,128)(2,1)}, f32[1360,128]{1,0:T(8,128)S(1)}, f32[1288,128]{1,0:T(8,128)S(1)}, f32[1280,128]{1,0:T(8,128)S(1)}, f32[16,128]{1,0:T(8,128)S(1)}) custom-call(f32[16,64,128]{2,1,0:T(8,128)S(1)} %get-tuple-element.24.p_ref, f32[16,64,128]{2,1,0:T(8,128)S(1)} %get-tuple-element.25.m_ref, ...), custom_call_target="tpu_custom_call" | custom-call | tf_op jit(solution)/shard_map/pallas_call | solution.py:42
  42.0 4.5 %all-to-all-start = ((bf16[16,272,128]{2,1,0:T(8,128)(2,1)}), bf16[16,272,128]{2,1,0:T(8,128)(2,1)S(1)}, u32[]{:S(2)}, u32[]{:S(2)}) async-start(bf16[16,272,128]{2,1,0:T(8,128)(2,1)} %get-tuple-element.31), calls=%async_computation | async-start | bytes 2228224 | tf_op jit(solution)/shard_map/all_to_all | solution.py:424
  46.5 2.3 %collective-permute-start.4 = (bf16[144,2048]{1,0:T(8,128)(2,1)}, bf16[144,2048]{1,0:T(8,128)(2,1)}, u32[]{:S(2)}, u32[]{:S(2)}) collective-permute-start(bf16[144,2048]{1,0:T(8,128)(2,1)} %get-tuple-element.32.x0_hbm), channel_id=1, source_target_pairs={{0,32},{32,0},{1,33},{33,1},{2,34},{34,2},{3,35},{35,3},{4,36},{36... | collective-permute-start | bytes 1769480 | tf_op jit(solution)/shard_map/ppermute | solution.py:421
  48.9 0.0 collective-permute-done.5.x2_hbm
  48.9 2.0 %collective-permute-start.6 = (bf16[144,2048]{1,0:T(8,128)(2,1)}, bf16[144,2048]{1,0:T(8,128)(2,1)}, u32[]{:S(2)}, u32[]{:S(2)}) collective-permute-start(bf16[144,2048]{1,0:T(8,128)(2,1)} %collective-permute-done.5.x2_hbm), channel_id=1, source_target_pairs={{0,32},{32,0},{1,33},{33,1},{2,34},{34,2},{3,35},{35,3},{4,36},{36... | collective-permute-start | bytes 1769480 | tf_op jit(solution)/shard_map/ppermute | solution.py:421
  50.9 0.0 collective-permute-done.4.x1_hbm
  50.9 12.8 %all-to-all-done.got_ref = bf16[16,272,128]{2,1,0:T(8,128)(2,1)S(1)} async-done(((bf16[16,272,128]{2,1,0:T(8,128)(2,1)}), bf16[16,272,128]{2,1,0:T(8,128)(2,1)S(1)}, u32[]{:S(2)}, u32[]{:S(2)}) %all-to-all-start) | async-done | bytes 1114144 | tf_op jit(solution)/shard_map/all_to_all | solution.py:424
  63.7 0.0 collective-permute-done.6.x3_hbm
  63.7 4.0 %shard_map.49 = f32[4,272,128]{2,1,0:T(8,128)S(1)} custom-call(s32[1]{0:T(128)} %bitcast.2.block_ref, bf16[16,272,128]{2,1,0:T(8,128)(2,1)S(1)} %all-to-all-done.got_ref, bf16[144,2048]{1,0:T(8,128)(2,1)} %get-tuple-element.32.x0_hbm, bf16[144,2048]{1,0:T(8,128)(2,1)} %collective-permute-done.4.x1_hbm, bf16[144,2048]{1,0:T(8,128)(2,1)} %collective-permute-done.5.x2_hbm, ...), custom_call_target="tpu_custom_call" | custom-call | tf_op jit(solution)/shard_map/pallas_call | solution.py:42
  67.7 11.5 %all_to_all.20.back_ref = f32[4,272,128]{2,1,0:T(8,128)S(1)} all-to-all(f32[4,272,128]{2,1,0:T(8,128)S(1)} %shard_map.49), channel_id=1, replica_groups=mesh['yl'=2,'x'=4,'c'=2,'yh'=2,'z'=16] {'yl','c'}, dimensions={0} | all-to-all | bytes 1114112 | tf_op jit(solution)/shard_map/all_to_all | solution.py:426
  79.2 1.6 %shard_map.50 = bf16[16,64,128]{2,1,0:T(8,128)(2,1)S(1)} custom-call(f32[4,272,128]{2,1,0:T(8,128)S(1)} %all_to_all.20.back_ref, f32[1360,128]{1,0:T(8,128)S(1)} %get-tuple-element.33.fz_ref, f32[1288,128]{1,0:T(8,128)S(1)} %get-tuple-element.34.fy_ref, f32[1280,128]{1,0:T(8,128)S(1)} %get-tuple-element.35.fx_ref, f32[16,128]{1,0:T(8,128)S(1)} %get-tuple-element.36.edge_ref), custom_call_target="tpu_custom_call" | custom-call | tf_op jit(solution)/shard_map/pallas_call | solution.py:42
  80.8 27.4 %all_to_all.21 = bf16[16,64,128]{2,1,0:T(8,128)(2,1)S(1)} all-to-all(bf16[16,64,128]{2,1,0:T(8,128)(2,1)S(1)} %shard_map.50), channel_id=1, replica_groups=mesh['yl'=2,'x'=4,'c'=2,'yh'=2,'z'=16] {'z'}, dimensions={0} | all-to-all | bytes 524288 | tf_op jit(solution)/shard_map/all_to_all | solution.py:429
  108.2 0.0 all-gather.2.cloned.1.call-done.y_hbm
  108.2 2.5 %collective-permute-start.7 = (bf16[1024,128]{1,0:T(8,128)(2,1)S(1)}, bf16[1024,128]{1,0:T(8,128)(2,1)S(1)}, u32[]{:S(2)}, u32[]{:S(2)}) collective-permute-start(bf16[1024,128]{1,0:T(8,128)(2,1)S(1)} %bitcast.5), channel_id=1, source_target_pairs={{0,16},{16,0},{1,17},{17,1},{2,18},{18,2},{3,19},{19,3},{4,20},{20... | collective-permute-start | bytes 786440 | tf_op jit(solution)/shard_map/ppermute | solution.py:431
  110.8 2.3 %shard_map.51 = (f32[1024,128]{1,0:T(8,128)S(1)}, bf16[1024,1024]{1,0:T(8,128)(2,1)S(1)}) custom-call(s32[1]{0:T(128)} %bitcast.side_ref, bf16[1024,2048]{1,0:T(8,128)(2,1)} %all-gather.2.cloned.1.call-done.y_hbm, bf16[1024,128]{1,0:T(8,128)(2,1)S(1)} %bitcast.6), custom_call_target="tpu_custom_call" | custom-call | tf_op jit(solution)/shard_map/pallas_call | solution.py:42
  113.1 4.9 %collective-permute-done.7.u_ref = bf16[1024,128]{1,0:T(8,128)(2,1)S(1)} collective-permute-done((bf16[1024,128]{1,0:T(8,128)(2,1)S(1)}, bf16[1024,128]{1,0:T(8,128)(2,1)S(1)}, u32[]{:S(2)}, u32[]{:S(2)}) %collective-permute-start.7) | collective-permute-done | bytes 262176 | tf_op jit(solution)/shard_map/ppermute | solution.py:431
  118.0 0.7 shard_map.52
  118.7 25.4 %all_to_all.22 = bf16[16,64,128]{2,1,0:T(8,128)(2,1)S(1)} all-to-all(bf16[16,64,128]{2,1,0:T(8,128)(2,1)S(1)} %bitcast.7), channel_id=1, replica_groups=mesh['yl'=2,'x'=4,'c'=2,'yh'=2,'z'=16] {'z'}, dimensions={0} | all-to-all | bytes 524288 | tf_op jit(solution)/shard_map/all_to_all | solution.py:434
  144.1 0.8 convert_element_type.3
Async XLA Ops:
  6.5 101.7 %all-gather.2.cloned.1.call-start = ((), (), s32[]{:S(2)}) async-start(), calls=%async_computation.4 | async-start | bytes 4325376 | tf_op jit(solution)/shard_map/all_gather | solution.py:416
  8.8 3.1 %collective-permute-start = (f32[48,128]{1,0:T(8,128)S(1)}, f32[48,128]{1,0:T(8,128)S(1)}, u32[]{:S(2)}, u32[]{:S(2)}) collective-permute-start(f32[48,128]{1,0:T(8,128)S(1)} %get-tuple-element.27.own_r_ref), channel_id=1, source_target_pairs={{0,32},{32,64},{64,96},{96,128},{128,160},{160,192},{192,224},{224... | collective-permute-start | bytes 73736 | tf_op jit(solution)/shard_map/ppermute | solution.py:403
  10.6 4.4 %collective-permute-start.1 = (f32[48,128]{1,0:T(8,128)S(1)}, f32[48,128]{1,0:T(8,128)S(1)}, u32[]{:S(2)}, u32[]{:S(2)}) collective-permute-start(f32[48,128]{1,0:T(8,128)S(1)} %get-tuple-element.26.own_l_ref), channel_id=1, source_target_pairs={{32,0},{64,32},{96,64},{128,96},{160,128},{192,160},{224,192},{256... | collective-permute-start | bytes 73736 | tf_op jit(solution)/shard_map/ppermute | solution.py:403
  15.7 33.1 %collective-permute-start.5 = (bf16[144,2048]{1,0:T(8,128)(2,1)}, bf16[144,2048]{1,0:T(8,128)(2,1)}, u32[]{:S(2)}, u32[]{:S(2)}) collective-permute-start(bf16[144,2048]{1,0:T(8,128)(2,1)} %get-tuple-element.32.x0_hbm), channel_id=1, source_target_pairs={{0,256},{256,0},{1,257},{257,1},{2,258},{258,2},{3,259},{259,3},{4... | collective-permute-start | bytes 1769480 | tf_op jit(solution)/shard_map/ppermute | solution.py:420
  22.0 14.4 %collective-permute-start.2 = (f32[7,16,128]{2,1,0:T(8,128)S(1)}, f32[7,16,128]{2,1,0:T(8,128)S(1)}, u32[]{:S(2)}, u32[]{:S(2)}) collective-permute-start(f32[7,16,128]{2,1,0:T(8,128)S(1)} %get-tuple-element.29), channel_id=1, source_target_pairs={{0,1},{1,2},{2,3},{3,4},{4,5},{5,6},{6,7},{7,8},{8,9},{9,10},{10,1... | collective-permute-start | bytes 172040 | tf_op jit(solution)/shard_map/ppermute | solution.py:403
  25.8 11.9 %collective-permute-start.3 = (f32[7,16,128]{2,1,0:T(8,128)S(1)}, f32[7,16,128]{2,1,0:T(8,128)S(1)}, u32[]{:S(2)}, u32[]{:S(2)}) collective-permute-start(f32[7,16,128]{2,1,0:T(8,128)S(1)} %get-tuple-element.30), channel_id=1, source_target_pairs={{1,0},{2,1},{3,2},{4,3},{5,4},{6,5},{7,6},{8,7},{9,8},{10,9},{11,1... | collective-permute-start | bytes 172040 | tf_op jit(solution)/shard_map/ppermute | solution.py:403
  42.0 21.7 %all-to-all-start = ((bf16[16,272,128]{2,1,0:T(8,128)(2,1)}), bf16[16,272,128]{2,1,0:T(8,128)(2,1)S(1)}, u32[]{:S(2)}, u32[]{:S(2)}) async-start(bf16[16,272,128]{2,1,0:T(8,128)(2,1)} %get-tuple-element.31), calls=%async_computation | async-start | bytes 2228224 | tf_op jit(solution)/shard_map/all_to_all | solution.py:424
  46.5 4.4 %collective-permute-start.4 = (bf16[144,2048]{1,0:T(8,128)(2,1)}, bf16[144,2048]{1,0:T(8,128)(2,1)}, u32[]{:S(2)}, u32[]{:S(2)}) collective-permute-start(bf16[144,2048]{1,0:T(8,128)(2,1)} %get-tuple-element.32.x0_hbm), channel_id=1, source_target_pairs={{0,32},{32,0},{1,33},{33,1},{2,34},{34,2},{3,35},{35,3},{4,36},{36... | collective-permute-start | bytes 1769480 | tf_op jit(solution)/shard_map/ppermute | solution.py:421
  48.9 14.8 %collective-permute-start.6 = (bf16[144,2048]{1,0:T(8,128)(2,1)}, bf16[144,2048]{1,0:T(8,128)(2,1)}, u32[]{:S(2)}, u32[]{:S(2)}) collective-permute-start(bf16[144,2048]{1,0:T(8,128)(2,1)} %collective-permute-done.5.x2_hbm), channel_id=1, source_target_pairs={{0,32},{32,0},{1,33},{33,1},{2,34},{34,2},{3,35},{35,3},{4,36},{36... | collective-permute-start | bytes 1769480 | tf_op jit(solution)/shard_map/ppermute | solution.py:421
  108.2 9.8 %collective-permute-start.7 = (bf16[1024,128]{1,0:T(8,128)(2,1)S(1)}, bf16[1024,128]{1,0:T(8,128)(2,1)S(1)}, u32[]{:S(2)}, u32[]{:S(2)}) collective-permute-start(bf16[1024,128]{1,0:T(8,128)(2,1)S(1)} %bitcast.5), channel_id=1, source_target_pairs={{0,16},{16,0},{1,17},{17,1},{2,18},{18,2},{3,19},{19,3},{4,20},{20... | collective-permute-start | bytes 786440 | tf_op jit(solution)/shard_map/ppermute | solution.py:431
Sparse Core Ops, SparseCore 0:
  9.4 78.5 all-gather.1
where the time goes:
time: 152 us
  blocking collectives  64.4 us (42%)
  starting transfers between devices  34.1 us (22%)
  waiting for transfers between devices  23.1 us (15%)
  Pallas kernels  15.9 us (10%)
  between operations  13.6 us (9%)
    all_to_all x1, blocking collectives, local(): mine = lax.all_to_all(updated, 'z', 0, 0, tiled=True).reshape(half, cx)  27.4 us
    all_to_all x1, blocking collectives, local(): out = lax.all_to_all(out, 'z', 0, 0, tiled=True)  25.4 us
    pallas_call x7, Pallas kernels, call(): pl.pallas_call(kernel, out_shape=out_shape, in_specs=[pl.BlockSpec(memory...  15.9 us
    all_to_all x1, waiting for transfers between devices, local(): got = lax.all_to_all(send, GX, 0, 0, tiled=True)  12.8 us
    all_to_all x1, blocking collectives, local(): back = lax.all_to_all(back, ('yl', 'c'), 0, 0, tiled=True)  11.5 us
    ppermute x2, starting transfers between devices, both_ways(): lax.ppermute(to_before, axis, [(j, i) for i, j in up])  10.9 us
    ppermute x1, starting transfers between devices, local(): rows_yl = lax.ppermute(rows, 'yl', swap)  6.26 us
    ppermute x2, starting transfers between devices, both_ways(): lax.ppermute(to_after, axis, up)  5.57 us
  transfers between devices with their start and end apart: 10, of which 5 were waited for; matrix products, arithmetic and copies ran while one was open for 0% of the time, Pallas kernels for 9%

commit v1 on v0

--- a/solution.py
+++ b/solution.py
@@ -62,7 +62,7 @@
     return lax.broadcasted_iota(jnp.int32, shape, axis)
 
 
-def pack_x_kernel(core_ref, p_hbm, m_hbm, x_hbm, y_hbm, left_ref, right_ref, p_ref, m_ref, rows_hbm, part_hbm, x_ref, part_ref, sems):
+def pack_x_kernel(core_ref, p_hbm, m_hbm, x_hbm, y_hbm, left_ref, right_ref, p_ref, m_ref, part_hbm, first_ref, last_ref, part_ref, sems):
     planes, _, cx = p_ref.shape
     pairs = planes // 2
     rows = part_hbm.shape[0]
@@ -70,7 +70,8 @@
         (y_hbm.at[pl.ds(pl.multiple_of(core_ref[0] * rows, rows), rows)], part_ref),
         (p_hbm, p_ref),
         (m_hbm, m_ref),
-        (x_hbm, x_ref),
+        (x_hbm.at[pl.ds(0, 16)], first_ref),
+        (x_hbm.at[pl.ds(cx - 16, 16)], last_ref),
     )
     copies = [pltpu.make_async_copy(src, dst, sems.at[i]) for i, (src, dst) in enumerate(copies)]
     for copy in copies:
@@ -78,9 +79,6 @@
     copies[0].wait()
     out = pltpu.make_async_copy(part_ref, part_hbm, sems.at[0])
     out.start()
-    copies[3].wait()
-    own = pltpu.make_async_copy(x_ref, rows_hbm.at[pl.ds(0, cx)], sems.at[3])
-    own.start()
     for a, ref in enumerate((p_ref, m_ref)):
         copies[1 + a].wait()
         for i in range(pairs):
@@ -90,13 +88,14 @@
                 left_ref[k : k + 1, :] = t[j : j + 1]
                 right_ref[k : k + 1, :] = t[cx - 2 + j : cx - 1 + j]
     base = 4 * pairs
-    first = x_ref[0:16, :][0:1].astype(F32)
-    last = x_ref[cx - 16 : cx, :][15:16].astype(F32)
+    copies[3].wait()
+    copies[4].wait()
+    first = first_ref[0:1, :].astype(F32)
+    last = last_ref[15:16, :].astype(F32)
     for s in range(16):
         left_ref[base + s : base + s + 1, :] = first[:, s * cx : (s + 1) * cx]
         right_ref[base + s : base + s + 1, :] = last[:, s * cx : (s + 1) * cx]
     out.wait()
-    own.wait()
 
 
 def strip(x, cy):
@@ -110,18 +109,24 @@
     return [strip(ref[k * pairs : (k + 1) * pairs, :], cy) for ref, k in refs]
 
 
-def pack_y_kernel(
-    p_ref, m_ref, own_l_ref, own_r_ref, left_ref, right_ref, _, up_ref, down_ref, rows_hbm, row_ref, cast_ref, sem
-):
-    planes, cy, cx = p_ref.shape
+def pack_rows_kernel(x_hbm, own_l_ref, own_r_ref, left_ref, right_ref, rows_hbm, row_ref, rows_ref, sem):
+    cx = x_hbm.shape[0]
+    come = pltpu.make_async_copy(x_hbm, rows_ref.at[pl.ds(0, cx)], sem)
+    come.start()
     base = left_ref.shape[0] - 16
     row_ref[...] = jnp.zeros(row_ref.shape, F32)
     for j, ref in enumerate((left_ref, own_l_ref, own_r_ref, right_ref)):
         for s in range(16):
-            row_ref[j : j + 1, s * cx : (s + 1) * cx] = ref[base + s : base + s + 1, :]
-    cast_ref[...] = row_ref[...].astype(BF16)
-    copy = pltpu.make_async_copy(cast_ref, rows_hbm.at[pl.ds(cx, 16)], sem)
-    copy.start()
+            row_ref[j : j + 1, s * 128 : (s + 1) * 128] = ref[base + s : base + s + 1, :]
+    rows_ref[cx:] = row_ref[...].astype(BF16)
+    come.wait()
+    leave = pltpu.make_async_copy(rows_ref, rows_hbm, sem)
+    leave.start()
+    leave.wait()
+
+
+def pack_y_kernel(p_ref, m_ref, left_ref, right_ref, up_ref, down_ref):
+    planes, cy, cx = p_ref.shape
     for a, ref in enumerate((p_ref, m_ref)):
         for r in range(3):
             up_ref[3 * a + r] = ref[:, cy - 3 + r, :]
@@ -137,7 +142,6 @@
             down = jnp.where(here, turn(s, at - OFF, 1), down)
     up_ref[6] = up
     down_ref[6] = down
-    copy.wait()
 
 
 def explicit_kernel(
@@ -265,9 +269,8 @@
     for copy in copies:
         copy.start()
     a = jnp.concatenate([got_ref[s] for s in range(parts)], axis=1)
-    for copy in copies:
-        copy.wait()
     for other, x_ref in enumerate((x0_ref, x1_ref, x2_ref, x3_ref)):
+        copies[other].wait()
         block = own ^ other
         m = lax.dot_general(a, x_ref[:cx], NT, preferred_element_type=F32)
         out_ref[block, : main + 8] = m[: main + 8]
@@ -340,18 +343,23 @@
     cx = p.shape[2]
     shape = (2 * p.shape[0] + 16, cx)
     cy, order = y_inverse.shape
-    out = (kept(shape, F32),) * 2 + (kept(p.shape, F32),) * 2 + (away_kept((cx + 16, order), BF16),)
-    out += (away_kept((cy // 2, order), BF16),)
-    scratch = (pltpu.VMEM((cx, order), BF16), pltpu.VMEM((cy // 2, order), BF16), pltpu.SemaphoreType.DMA((4,)))
-    return call(pack_x_kernel, out, (p, m, x_inverse, y_inverse), core, scratch, range(4), (4, 5))
-
-
-def pack_y(p, m, own_l, own_r, left, right, rows):
-    order = rows.shape[1]
-    out = (kept((7, p.shape[0], p.shape[2]), F32),) * 2 + (away_kept(rows.shape, BF16),)
-    scratch = (pltpu.VMEM((16, order), F32), pltpu.VMEM((16, order), BF16), pltpu.SemaphoreType.DMA(()))
-    args = (p, m, own_l, own_r, left, right, rows)
-    return call(pack_y_kernel, out, args, scratch=scratch, far=(6,), far_out=(2,), aliases={6: 2})
+    out = (kept(shape, F32),) * 2 + (kept(p.shape, F32),) * 2 + (away_kept((cy // 2, order), BF16),)
+    few = pltpu.VMEM((16, order), BF16)
+    scratch = (few, few, pltpu.VMEM((cy // 2, order), BF16), pltpu.SemaphoreType.DMA((5,)))
+    return call(pack_x_kernel, out, (p, m, x_inverse, y_inverse), core, scratch, range(4), (4,))
+
+
+def pack_rows(x_inverse, own_l, own_r, left, right):
+    cx, order = x_inverse.shape
+    shape = (cx + 16, order)
+    scratch = (pltpu.VMEM((16, order), F32), pltpu.VMEM(shape, BF16), pltpu.SemaphoreType.DMA(()))
+    args = (x_inverse, own_l, own_r, left, right)
+    return call(pack_rows_kernel, (away_kept(shape, BF16),), args, scratch=scratch, far=(0,), far_out=(0,))[0]
+
+
+def pack_y(p, m, left, right):
+    out = (kept((7, p.shape[0], p.shape[2]), F32),) * 2
+    return call(pack_y_kernel, out, (p, m, left, right))
 
 
 def explicit(*args):
@@ -412,11 +420,12 @@
 
     one = lambda v: v.reshape(1).astype(jnp.int32)
 
-    own_l, own_r, phase_field, mobility, rows, y_part = pack_x(one(core), phase_field, mobility, x_inverse, y_inverse)
+    own_l, own_r, phase_field, mobility, y_part = pack_x(one(core), phase_field, mobility, x_inverse, y_inverse)
     y_rows = lax.all_gather(y_part, ("z", "c"), axis=0, tiled=True)
     left, right = both_ways(own_l, own_r, GX)
-    to_up, to_down, rows = pack_y(phase_field, mobility, own_l, own_r, left, right, rows)
+    to_up, to_down = pack_y(phase_field, mobility, left, right)
     up, down = both_ways(to_down, to_up, GY)
+    rows = pack_rows(x_inverse, own_l, own_r, left, right)
     rows_yl = lax.ppermute(rows, "yl", swap)
     x_blocks = (rows, lax.ppermute(rows, "c", swap), rows_yl, lax.ppermute(rows_yl, "c", swap))
 

time: 152 us -> 153 us (level)
  the two profiles are of different devices: /device:TPU:16 before, /device:TPU:32 now
where the time goes in v1:
time: 153 us
  blocking collectives  69.2 us (45%)
  starting transfers between devices  27.9 us (18%)
  waiting for transfers between devices  24.8 us (16%)
  Pallas kernels  16.5 us (11%)
  between operations  13.6 us (9%)
    all_to_all x1, blocking collectives, local(): mine = lax.all_to_all(updated, 'z', 0, 0, tiled=True).reshape(half, cx)  33.5 us
    all_to_all x1, blocking collectives, local(): out = lax.all_to_all(out, 'z', 0, 0, tiled=True)  24.2 us
    pallas_call x8, Pallas kernels, call(): pl.pallas_call(kernel, out_shape=out_shape, in_specs=[pl.BlockSpec(memory...  16.5 us
    all_to_all x1, waiting for transfers between devices, local(): got = lax.all_to_all(send, GX, 0, 0, tiled=True)  12.7 us
    all_to_all x1, blocking collectives, local(): back = lax.all_to_all(back, ('yl', 'c'), 0, 0, tiled=True)  11.5 us
    ppermute x2, waiting for transfers between devices, both_ways(): lax.ppermute(to_before, axis, [(j, i) for i, j in up])  7.8 us
    ppermute x1, starting transfers between devices, local(): rows_yl = lax.ppermute(rows, 'yl', swap)  6.56 us
    ppermute x2, starting transfers between devices, both_ways(): lax.ppermute(to_after, axis, up)  5.57 us
  transfers between devices with their start and end apart: 10, of which 5 were waited for; matrix products, arithmetic and copies ran while one was open for 0% of the time, Pallas kernels for 9%

profile of v1, /device:TPU:32, one launch (start us, length us, event | category | flops | bytes accessed | tf_op | source)
XLA Modules:
  0.0 152.8 jit_solution(17320299259278182952)
XLA Ops:
  6.5 0.0 all-gather.2.cloned.1.call-start
  6.5 1.6 %shard_map.46 = (f32[48,128]{1,0:T(8,128)S(1)}, f32[48,128]{1,0:T(8,128)S(1)}, f32[16,64,128]{2,1,0:T(8,128)S(1)}, f32[16,64,128]{2,1,0:T(8,128)S(1)}, bf16[32,2048]{1,0:T(8,128)(2,1)}) custom-call(s32[1]{0:T(128)} %bitcast.1.core_ref, f32[16,64,128]{2,1,0:T(8,128)} %p_hbm.1, f32[16,64,128]{2,1,0:T(8,128)} %m_hbm.1, bf16[128,2048]{1,0:T(8,128)(2,1)} %x_hbm.3, ...), custom_call_target="tpu_custom_call" | custom-call | tf_op jit(solution)/shard_map/pallas_call | solution.py:42
  8.1 0.0 all-gather.2.cloned.1.call-update
  8.2 1.7 %collective-permute-start = (f32[48,128]{1,0:T(8,128)S(1)}, f32[48,128]{1,0:T(8,128)S(1)}, u32[]{:S(2)}, u32[]{:S(2)}) collective-permute-start(f32[48,128]{1,0:T(8,128)S(1)} %get-tuple-element.25.own_r_ref), channel_id=1, source_target_pairs={{0,32},{32,64},{64,96},{96,128},{128,160},{160,192},{192,224},{224... | collective-permute-start | bytes 73736 | tf_op jit(solution)/shard_map/ppermute | solution.py:411
  9.9 1.3 collective-permute-start.1
  11.2 0.0 collective-permute-done.left_ref
  11.2 3.1 %collective-permute-done.1.right_ref = f32[48,128]{1,0:T(8,128)S(1)} collective-permute-done((f32[48,128]{1,0:T(8,128)S(1)}, f32[48,128]{1,0:T(8,128)S(1)}, u32[]{:S(2)}, u32[]{:S(2)}) %collective-permute-start.1) | collective-permute-done | bytes 24608 | tf_op jit(solution)/shard_map/ppermute | solution.py:411
  14.3 1.9 %shard_map.49.x0_hbm = bf16[144,2048]{1,0:T(8,128)(2,1)} custom-call(bf16[128,2048]{1,0:T(8,128)(2,1)} %x_hbm.3, f32[48,128]{1,0:T(8,128)S(1)} %get-tuple-element.24.own_l_ref, f32[48,128]{1,0:T(8,128)S(1)} %get-tuple-element.25.own_r_ref, f32[48,128]{1,0:T(8,128)S(1)} %collective-permute-done.left_ref, f32[48,128]{1,0:T(8,128)S(1)} %collective-permute-done.1.right_ref), custom_call_target="tpu_custom_call" | custom-call | tf_op jit(solution)/shard_map/pallas_call | solution.py:42
  16.2 6.6 %collective-permute-start.5 = (bf16[144,2048]{1,0:T(8,128)(2,1)}, bf16[144,2048]{1,0:T(8,128)(2,1)}, u32[]{:S(2)}, u32[]{:S(2)}) collective-permute-start(bf16[144,2048]{1,0:T(8,128)(2,1)} %shard_map.49.x0_hbm), channel_id=1, source_target_pairs={{0,256},{256,0},{1,257},{257,1},{2,258},{258,2},{3,259},{259,3},{4... | collective-permute-start | bytes 1769480 | tf_op jit(solution)/shard_map/ppermute | solution.py:429
  22.7 0.2 shard_map.47
  22.9 3.8 %collective-permute-start.2 = (f32[7,16,128]{2,1,0:T(8,128)S(1)}, f32[7,16,128]{2,1,0:T(8,128)S(1)}, u32[]{:S(2)}, u32[]{:S(2)}) collective-permute-start(f32[7,16,128]{2,1,0:T(8,128)S(1)} %get-tuple-element.26), channel_id=1, source_target_pairs={{0,1},{1,2},{2,3},{3,4},{4,5},{5,6},{6,7},{7,8},{8,9},{9,10},{10,1... | collective-permute-start | bytes 172040 | tf_op jit(solution)/shard_map/ppermute | solution.py:411
  26.7 2.0 %collective-permute-start.3 = (f32[7,16,128]{2,1,0:T(8,128)S(1)}, f32[7,16,128]{2,1,0:T(8,128)S(1)}, u32[]{:S(2)}, u32[]{:S(2)}) collective-permute-start(f32[7,16,128]{2,1,0:T(8,128)S(1)} %get-tuple-element.27), channel_id=1, source_target_pairs={{1,0},{2,1},{3,2},{4,3},{5,4},{6,5},{7,6},{8,7},{9,8},{10,9},{11,1... | collective-permute-start | bytes 172040 | tf_op jit(solution)/shard_map/ppermute | solution.py:411
  28.8 0.2 collective-permute-done.2.up_ref
  29.0 4.7 %collective-permute-done.3.down_ref = f32[7,16,128]{2,1,0:T(8,128)S(1)} collective-permute-done((f32[7,16,128]{2,1,0:T(8,128)S(1)}, f32[7,16,128]{2,1,0:T(8,128)S(1)}, u32[]{:S(2)}, u32[]{:S(2)}) %collective-permute-start.3) | collective-permute-done | bytes 57376 | tf_op jit(solution)/shard_map/ppermute | solution.py:411
  33.7 4.3 %shard_map.48 = (bf16[16,272,128]{2,1,0:T(8,128)(2,1)}, f32[1360,128]{1,0:T(8,128)S(1)}, f32[1288,128]{1,0:T(8,128)S(1)}, f32[1280,128]{1,0:T(8,128)S(1)}, f32[16,128]{1,0:T(8,128)S(1)}) custom-call(f32[16,64,128]{2,1,0:T(8,128)S(1)} %get-tuple-element.22.p_ref, f32[16,64,128]{2,1,0:T(8,128)S(1)} %get-tuple-element.23.m_ref, ...), custom_call_target="tpu_custom_call" | custom-call | tf_op jit(solution)/shard_map/pallas_call | solution.py:42
  38.0 3.7 %all-to-all-start = ((bf16[16,272,128]{2,1,0:T(8,128)(2,1)}), bf16[16,272,128]{2,1,0:T(8,128)(2,1)S(1)}, u32[]{:S(2)}, u32[]{:S(2)}) async-start(bf16[16,272,128]{2,1,0:T(8,128)(2,1)} %get-tuple-element.28), calls=%async_computation | async-start | bytes 2228224 | tf_op jit(solution)/shard_map/all_to_all | solution.py:433
  41.7 2.3 %collective-permute-start.4 = (bf16[144,2048]{1,0:T(8,128)(2,1)}, bf16[144,2048]{1,0:T(8,128)(2,1)}, u32[]{:S(2)}, u32[]{:S(2)}) collective-permute-start(bf16[144,2048]{1,0:T(8,128)(2,1)} %shard_map.49.x0_hbm), channel_id=1, source_target_pairs={{0,32},{32,0},{1,33},{33,1},{2,34},{34,2},{3,35},{35,3},{4,36},{36... | collective-permute-start | bytes 1769480 | tf_op jit(solution)/shard_map/ppermute | solution.py:430
  44.0 0.0 collective-permute-done.5.x2_hbm
  44.0 2.1 %collective-permute-start.6 = (bf16[144,2048]{1,0:T(8,128)(2,1)}, bf16[144,2048]{1,0:T(8,128)(2,1)}, u32[]{:S(2)}, u32[]{:S(2)}) collective-permute-start(bf16[144,2048]{1,0:T(8,128)(2,1)} %collective-permute-done.5.x2_hbm), channel_id=1, source_target_pairs={{0,32},{32,0},{1,33},{33,1},{2,34},{34,2},{3,35},{35,3},{4,36},{36... | collective-permute-start | bytes 1769480 | tf_op jit(solution)/shard_map/ppermute | solution.py:430
  46.1 0.0 collective-permute-done.4.x1_hbm
  46.1 12.7 %all-to-all-done.got_ref = bf16[16,272,128]{2,1,0:T(8,128)(2,1)S(1)} async-done(((bf16[16,272,128]{2,1,0:T(8,128)(2,1)}), bf16[16,272,128]{2,1,0:T(8,128)(2,1)S(1)}, u32[]{:S(2)}, u32[]{:S(2)}) %all-to-all-start) | async-done | bytes 1114144 | tf_op jit(solution)/shard_map/all_to_all | solution.py:433
  58.8 0.0 collective-permute-done.6.x3_hbm
  58.8 4.0 %shard_map.50 = f32[4,272,128]{2,1,0:T(8,128)S(1)} custom-call(s32[1]{0:T(128)} %bitcast.2.block_ref, bf16[16,272,128]{2,1,0:T(8,128)(2,1)S(1)} %all-to-all-done.got_ref, bf16[144,2048]{1,0:T(8,128)(2,1)} %shard_map.49.x0_hbm, bf16[144,2048]{1,0:T(8,128)(2,1)} %collective-permute-done.4.x1_hbm, bf16[144,2048]{1,0:T(8,128)(2,1)} %collective-permute-done.5.x2_hbm, ...), custom_call_target="tpu_custom_call" | custom-call | tf_op jit(solution)/shard_map/pallas_call | solution.py:42
  62.8 11.5 %all_to_all.20.back_ref = f32[4,272,128]{2,1,0:T(8,128)S(1)} all-to-all(f32[4,272,128]{2,1,0:T(8,128)S(1)} %shard_map.50), channel_id=1, replica_groups=mesh['yl'=2,'x'=4,'c'=2,'yh'=2,'z'=16] {'yl','c'}, dimensions={0} | all-to-all | bytes 1114112 | tf_op jit(solution)/shard_map/all_to_all | solution.py:435
  74.4 1.6 %shard_map.51 = bf16[16,64,128]{2,1,0:T(8,128)(2,1)S(1)} custom-call(f32[4,272,128]{2,1,0:T(8,128)S(1)} %all_to_all.20.back_ref, f32[1360,128]{1,0:T(8,128)S(1)} %get-tuple-element.29.fz_ref, f32[1288,128]{1,0:T(8,128)S(1)} %get-tuple-element.30.fy_ref, f32[1280,128]{1,0:T(8,128)S(1)} %get-tuple-element.31.fx_ref, f32[16,128]{1,0:T(8,128)S(1)} %get-tuple-element.32.edge_ref), custom_call_target="tpu_custom_call" | custom-call | tf_op jit(solution)/shard_map/pallas_call | solution.py:42
  75.9 33.5 %all_to_all.21 = bf16[16,64,128]{2,1,0:T(8,128)(2,1)S(1)} all-to-all(bf16[16,64,128]{2,1,0:T(8,128)(2,1)S(1)} %shard_map.51), channel_id=1, replica_groups=mesh['yl'=2,'x'=4,'c'=2,'yh'=2,'z'=16] {'z'}, dimensions={0} | all-to-all | bytes 524288 | tf_op jit(solution)/shard_map/all_to_all | solution.py:438
  109.4 4.5 %collective-permute-start.7 = (bf16[1024,128]{1,0:T(8,128)(2,1)S(1)}, bf16[1024,128]{1,0:T(8,128)(2,1)S(1)}, u32[]{:S(2)}, u32[]{:S(2)}) collective-permute-start(bf16[1024,128]{1,0:T(8,128)(2,1)S(1)} %bitcast.5), channel_id=1, source_target_pairs={{0,16},{16,0},{1,17},{17,1},{2,18},{18,2},{3,19},{19,3},{4,20},{20... | collective-permute-start | bytes 786440 | tf_op jit(solution)/shard_map/ppermute | solution.py:440
  113.9 2.3 %shard_map.52 = (f32[1024,128]{1,0:T(8,128)S(1)}, bf16[1024,1024]{1,0:T(8,128)(2,1)S(1)}) custom-call(s32[1]{0:T(128)} %bitcast.side_ref, bf16[1024,2048]{1,0:T(8,128)(2,1)} %all-gather.2.cloned.1.call-done.y_hbm, bf16[1024,128]{1,0:T(8,128)(2,1)S(1)} %bitcast.6), custom_call_target="tpu_custom_call" | custom-call | tf_op jit(solution)/shard_map/pallas_call | solution.py:42
  116.2 4.0 %collective-permute-done.7.u_ref = bf16[1024,128]{1,0:T(8,128)(2,1)S(1)} collective-permute-done((bf16[1024,128]{1,0:T(8,128)(2,1)S(1)}, bf16[1024,128]{1,0:T(8,128)(2,1)S(1)}, u32[]{:S(2)}, u32[]{:S(2)}) %collective-permute-start.7) | collective-permute-done | bytes 262176 | tf_op jit(solution)/shard_map/ppermute | solution.py:440
  120.2 0.7 shard_map.53
  120.9 24.2 %all_to_all.22 = bf16[16,64,128]{2,1,0:T(8,128)(2,1)S(1)} all-to-all(bf16[16,64,128]{2,1,0:T(8,128)(2,1)S(1)} %bitcast.7), channel_id=1, replica_groups=mesh['yl'=2,'x'=4,'c'=2,'yh'=2,'z'=16] {'z'}, dimensions={0} | all-to-all | bytes 524288 | tf_op jit(solution)/shard_map/all_to_all | solution.py:443
  145.1 0.8 convert_element_type.3
  (1 shorter events, 0.0 us)
Async XLA Ops:
  6.5 102.9 %all-gather.2.cloned.1.call-start = ((), (), s32[]{:S(2)}) async-start(), calls=%async_computation.4 | async-start | bytes 4325376 | tf_op jit(solution)/shard_map/all_gather | solution.py:424
  8.2 3.1 %collective-permute-start = (f32[48,128]{1,0:T(8,128)S(1)}, f32[48,128]{1,0:T(8,128)S(1)}, u32[]{:S(2)}, u32[]{:S(2)}) collective-permute-start(f32[48,128]{1,0:T(8,128)S(1)} %get-tuple-element.25.own_r_ref), channel_id=1, source_target_pairs={{0,32},{32,64},{64,96},{96,128},{128,160},{160,192},{192,224},{224... | collective-permute-start | bytes 73736 | tf_op jit(solution)/shard_map/ppermute | solution.py:411
  9.9 4.4 %collective-permute-start.1 = (f32[48,128]{1,0:T(8,128)S(1)}, f32[48,128]{1,0:T(8,128)S(1)}, u32[]{:S(2)}, u32[]{:S(2)}) collective-permute-start(f32[48,128]{1,0:T(8,128)S(1)} %get-tuple-element.24.own_l_ref), channel_id=1, source_target_pairs={{32,0},{64,32},{96,64},{128,96},{160,128},{192,160},{224,192},{256... | collective-permute-start | bytes 73736 | tf_op jit(solution)/shard_map/ppermute | solution.py:411
  16.2 27.8 %collective-permute-start.5 = (bf16[144,2048]{1,0:T(8,128)(2,1)}, bf16[144,2048]{1,0:T(8,128)(2,1)}, u32[]{:S(2)}, u32[]{:S(2)}) collective-permute-start(bf16[144,2048]{1,0:T(8,128)(2,1)} %shard_map.49.x0_hbm), channel_id=1, source_target_pairs={{0,256},{256,0},{1,257},{257,1},{2,258},{258,2},{3,259},{259,3},{4... | collective-permute-start | bytes 1769480 | tf_op jit(solution)/shard_map/ppermute | solution.py:429
  22.9 6.1 %collective-permute-start.2 = (f32[7,16,128]{2,1,0:T(8,128)S(1)}, f32[7,16,128]{2,1,0:T(8,128)S(1)}, u32[]{:S(2)}, u32[]{:S(2)}) collective-permute-start(f32[7,16,128]{2,1,0:T(8,128)S(1)} %get-tuple-element.26), channel_id=1, source_target_pairs={{0,1},{1,2},{2,3},{3,4},{4,5},{5,6},{6,7},{7,8},{8,9},{9,10},{10,1... | collective-permute-start | bytes 172040 | tf_op jit(solution)/shard_map/ppermute | solution.py:411
  26.7 7.0 %collective-permute-start.3 = (f32[7,16,128]{2,1,0:T(8,128)S(1)}, f32[7,16,128]{2,1,0:T(8,128)S(1)}, u32[]{:S(2)}, u32[]{:S(2)}) collective-permute-start(f32[7,16,128]{2,1,0:T(8,128)S(1)} %get-tuple-element.27), channel_id=1, source_target_pairs={{1,0},{2,1},{3,2},{4,3},{5,4},{6,5},{7,6},{8,7},{9,8},{10,9},{11,1... | collective-permute-start | bytes 172040 | tf_op jit(solution)/shard_map/ppermute | solution.py:411
  38.0 20.8 %all-to-all-start = ((bf16[16,272,128]{2,1,0:T(8,128)(2,1)}), bf16[16,272,128]{2,1,0:T(8,128)(2,1)S(1)}, u32[]{:S(2)}, u32[]{:S(2)}) async-start(bf16[16,272,128]{2,1,0:T(8,128)(2,1)} %get-tuple-element.28), calls=%async_computation | async-start | bytes 2228224 | tf_op jit(solution)/shard_map/all_to_all | solution.py:433
  41.7 4.4 %collective-permute-start.4 = (bf16[144,2048]{1,0:T(8,128)(2,1)}, bf16[144,2048]{1,0:T(8,128)(2,1)}, u32[]{:S(2)}, u32[]{:S(2)}) collective-permute-start(bf16[144,2048]{1,0:T(8,128)(2,1)} %shard_map.49.x0_hbm), channel_id=1, source_target_pairs={{0,32},{32,0},{1,33},{33,1},{2,34},{34,2},{3,35},{35,3},{4,36},{36... | collective-permute-start | bytes 1769480 | tf_op jit(solution)/shard_map/ppermute | solution.py:430
  44.0 14.8 %collective-permute-start.6 = (bf16[144,2048]{1,0:T(8,128)(2,1)}, bf16[144,2048]{1,0:T(8,128)(2,1)}, u32[]{:S(2)}, u32[]{:S(2)}) collective-permute-start(bf16[144,2048]{1,0:T(8,128)(2,1)} %collective-permute-done.5.x2_hbm), channel_id=1, source_target_pairs={{0,32},{32,0},{1,33},{33,1},{2,34},{34,2},{3,35},{35,3},{4,36},{36... | collective-permute-start | bytes 1769480 | tf_op jit(solution)/shard_map/ppermute | solution.py:430
  109.4 10.8 %collective-permute-start.7 = (bf16[1024,128]{1,0:T(8,128)(2,1)S(1)}, bf16[1024,128]{1,0:T(8,128)(2,1)S(1)}, u32[]{:S(2)}, u32[]{:S(2)}) collective-permute-start(bf16[1024,128]{1,0:T(8,128)(2,1)S(1)} %bitcast.5), channel_id=1, source_target_pairs={{0,16},{16,0},{1,17},{17,1},{2,18},{18,2},{3,19},{19,3},{4,20},{20... | collective-permute-start | bytes 786440 | tf_op jit(solution)/shard_map/ppermute | solution.py:440
Sparse Core Ops, SparseCore 0:
  9.4 77.6 all-gather.1
